TPU v7x, 256 devices: a whole 4x4x8 slice. The times are simulated.
256 devices in a mesh: ctx: 32 (over z, y), tp: 8 (over x, core).
Axes of the slice: x: 4, y: 4, z: 8, core: 2. Of those that a mesh axis runs over, the one named last changes fastest.
Arguments:
- tokens: bfloat16 [24576, 4096], P(('ctx', 'tp')), may hold values from -6 to 6
- norm_gain: float32 [4096], replicated, may hold values from 0.1 to 1.9
- w_qkv: bfloat16 [4096, 8192], P('ctx', 'tp'), may hold values from -0.09375 to 0.09375
- w_out: bfloat16 [4096, 4096], P('tp', 'ctx'), may hold values from -0.09375 to 0.09375
- head_gain: float32 [4096], P('tp'), may hold values from 0.1 to 1.9
- input_codes: int32 [8, 24576], P('tp', 'ctx'), may hold values from -4 to 4
- forget_codes: int32 [8, 24576], P('tp', 'ctx'), may hold values from -24 to 4
- forget_bias: float32 [8], P('tp'), may hold values from 3 to 13.5, as said below
- document_begin_flags: int32 [24576], P('ctx'), may hold values 0 or 1
Outputs:
- mixed: bfloat16 [24576, 4096], P(('ctx', 'tp'))
Inputs may be any that keep to these rules, and one draw needn't show every extreme that they name: `forget_bias`: a bias for each head.
All inputs are finite; a program needn't handle non-finite values. No bound on the sum of `document_begin_flags` on one device may be relied on, other than what follows from the above.
Results may differ from a plain program's by a relative error of at most 0.017.
Values may be sent and summed in bfloat16 or wider, within the bound.
A program may use at most 64 MiB of HBM per device.

v0:
```python
import jax
import jax.numpy as jnp
from jax import lax
from jax.sharding import PartitionSpec as P

DK = 256
DV = 512
EPSILON = 1e-06
FORGET_STEP = 0.5
INPUT_STEP = 0.5


def carried_in(shard, axis, combine, identity):
    count, position = (lax.axis_size(axis), lax.axis_index(axis))
    everything = jax.tree.map(
        lambda part, kind: lax.all_gather(part.astype(kind), axis),
        shard,
        (jnp.bfloat16, jnp.bfloat16),
    )
    start = jax.tree.map(
        lambda part, zero: jnp.broadcast_to(jnp.asarray(zero, part.dtype), part.shape),
        shard,
        identity,
    )

    def hop(k, before):
        reached = k < position
        new = combine(
            before, jax.tree.map(lambda part, own: part[k].astype(own.dtype), everything, shard)
        )
        return jax.tree.map(lambda a, b: jnp.where(reached, a, b), new, before)

    return lax.fori_loop(0, count, hop, start)


def rms_rows(embedded_entries, norm_gain):
    token_float = embedded_entries.astype(jnp.float32)
    moment = jnp.mean(token_float * token_float, axis=1, keepdims=True)
    return (token_float * lax.rsqrt(moment + EPSILON) * norm_gain).astype(jnp.bfloat16)


def local_terms(queries, key_rows, values, log_forget, input_gate, starts):
    length = queries.shape[0]
    scaling = queries.shape[1] ** (-0.5)
    segment = jnp.cumsum(starts)
    levels = jnp.cumsum(log_forget)
    position = jnp.arange(length)
    allowed = (position[:, None] >= position[None, :]) & (segment[:, None] == segment[None, :])
    decays = jnp.where(
        allowed,
        jnp.exp(jnp.minimum(levels[:, None] - levels[None, :], 0.0) + input_gate[None, :]),
        0.0,
    )
    scores = jnp.dot(queries, key_rows.T, preferred_element_type=jnp.float32) * scaling
    weights = (scores * decays).astype(jnp.bfloat16)
    inner_part = jnp.dot(weights, values, preferred_element_type=jnp.float32)
    last_level = levels[-1]
    last_seg = segment[-1]
    keeping = jnp.where(segment == last_seg, jnp.exp(last_level - levels + input_gate), 0.0)
    weighted = (key_rows.astype(jnp.float32) * keeping[:, None]).astype(jnp.bfloat16)
    local_state = lax.dot_general(
        weighted, values, (((0,), (0,)), ((), ())), preferred_element_type=jnp.float32
    )
    passing = jnp.where(last_seg == 0, jnp.exp(last_level), 0.0)
    carried = jnp.where(segment == 0, jnp.exp(levels), 0.0) * scaling
    return (inner_part, local_state, passing, carried)


def apply_state(queries, carried, incoming):
    lifted = queries.astype(jnp.float32) * carried[:, None]
    return jnp.dot(
        lifted, incoming, precision=lax.Precision.HIGHEST, preferred_element_type=jnp.float32
    )


def head_norm(head_out, gain):
    centre = jnp.mean(head_out, axis=1, keepdims=True)
    shifted = head_out - centre
    spread = jnp.mean(shifted * shifted, axis=1, keepdims=True)
    return (shifted * lax.rsqrt(spread + EPSILON) * gain).astype(jnp.bfloat16)


def combine(earlier, later):
    return (earlier[0] * later[0], later[0][:, None, None] * earlier[1] + later[1])


def local(
    tokens,
    norm_gain,
    w_qkv,
    w_out,
    head_gain,
    input_codes,
    forget_codes,
    forget_bias,
    document_begin_flags,
):
    normed = rms_rows(tokens, norm_gain)
    every_row_list = lax.all_gather(normed, "tp", axis=0, tiled=True)
    parameter_collection = lax.all_gather(w_qkv, "ctx", axis=0, tiled=True)
    rows_combined = jnp.dot(
        every_row_list, parameter_collection, preferred_element_type=jnp.float32
    )
    rows_combined = rows_combined.astype(jnp.bfloat16)
    heads_here = forget_bias.shape[0]
    stride = 2 * DK + DV
    query_list, inner_list, state_list, passing_list, carried_list = ([], [], [], [], [])
    attention_slot_number = 0
    offset = attention_slot_number * stride
    queries = rows_combined[:, offset : offset + DK]
    key_rows = rows_combined[:, offset + DK : offset + 2 * DK]
    values = rows_combined[:, offset + 2 * DK : offset + stride]
    log_forget = jax.nn.log_sigmoid(
        FORGET_STEP * forget_codes[attention_slot_number].astype(jnp.float32)
        + forget_bias[attention_slot_number]
    )
    input_gate = INPUT_STEP * input_codes[attention_slot_number].astype(jnp.float32)
    inner_part, local_state, passing, carried = local_terms(
        queries, key_rows, values, log_forget, input_gate, document_begin_flags
    )
    query_list.append(queries)
    inner_list.append(inner_part)
    state_list.append(local_state)
    passing_list.append(passing)
    carried_list.append(carried)
    identity = (jnp.ones((heads_here,), jnp.float32), jnp.zeros((heads_here, DK, DV), jnp.float32))
    scanned = carried_in((jnp.stack(passing_list), jnp.stack(state_list)), "ctx", combine, identity)
    incoming = scanned[1]
    attention_slot_number = 0
    head_out = inner_list[attention_slot_number] + apply_state(
        query_list[attention_slot_number],
        carried_list[attention_slot_number],
        incoming[attention_slot_number],
    )
    normed_heads = head_norm(head_out, head_gain)
    out_columns = lax.all_gather(w_out, "ctx", axis=1, tiled=True)
    summed = lax.psum_scatter(
        jnp.dot(normed_heads, out_columns, preferred_element_type=jnp.float32).astype(jnp.bfloat16),
        "tp",
        scatter_dimension=0,
        tiled=True,
    ).astype(jnp.float32)
    return (tokens.astype(jnp.float32) + summed).astype(jnp.bfloat16)


def solution(mesh):
    placed = (
        P(("ctx", "tp"), None),
        P(),
        P("ctx", "tp"),
        P("tp", "ctx"),
        P("tp"),
        P("tp", "ctx"),
        P("tp", "ctx"),
        P("tp"),
        P("ctx"),
    )
    return jax.shard_map(
        local, mesh=mesh, in_specs=placed, out_specs=P(("ctx", "tp"), None), check_vma=False
    )
```

profile of v0, /device:TPU:1, one launch (start us, length us, event | category | flops | bytes accessed | tf_op | source)
XLA Modules:
  0.0 411.1 jit_solution(12727475956866767131)
XLA Ops:
  6.5 1.4 fusion.2
  8.0 2.3 fusion.4
  14.2 1.3 exponential_select_fusion
  15.5 42.6 %all-gather.6.cloned.1.call-done = bf16[768,4096]{1,0:T(8,128)(2,1)} async-done(((bf16[96,4096]{1,0:T(8,128)(2,1)}), bf16[768,4096]{1,0:T(8,128)(2,1)}) %all-gather.6.cloned.1.call-update) | async-done | bytes 6291472 | tf_op jit(solution)/shard_map/all_gather | solution.py:99
  58.1 100.4 %all-gather.8.cloned.1.call-done = bf16[4096,1024]{1,0:T(8,128)(2,1)} async-done(((bf16[128,1024]{1,0:T(8,128)(2,1)}), bf16[4096,1024]{1,0:T(8,128)(2,1)}) %all-gather.8.cloned.1.call-update) | async-done | bytes 8388624 | tf_op jit(solution)/shard_map/all_gather | solution.py:100
  158.5 10.9 %convolution_convert_fusion.1 = bf16[768,1024]{1,0:T(8,128)(2,1)S(1)} fusion(bf16[768,4096]{1,0:T(8,128)(2,1)} %all-gather.6.cloned.1.call-done, bf16[4096,1024]{1,0:T(8,128)(2,1)} %all-gather.8.cloned.1.call-done), kind=kOutput, calls=%fused_computation.10 | convolution fusion | flops 6443237376 | bytes 16252928 | tf_op jit(solution)/shard_map/dot_general | solution.py:101
  169.5 1.3 convolution_convert_fusion.2
  173.5 0.7 dynamic-update-slice
  174.2 57.4 %all-reduce = bf16[32]{0:T(256)(128)(2,1)S(1)} all-reduce(bf16[32]{0:T(256)(128)(2,1)S(1)} %dynamic-update-slice), channel_id=1, replica_groups=mesh['ctx'=32,'tp'=8] {'ctx'}, use_global_device_ids=true, to_apply=%add | all-reduce | flops 32 | bytes 128
  231.6 2.5 fusion.6
  234.2 32.5 %all-gather.12.cloned.1.call-done = bf16[8192,512]{1,0:T(8,128)(2,1)} async-done(((bf16[256,512]{1,0:T(8,128)(2,1)}), bf16[8192,512]{1,0:T(8,128)(2,1)}) %all-gather.12.cloned.1.call-update) | async-done | bytes 8388624 | tf_op jit(solution)/shard_map/all_gather | solution.py:16
  266.7 81.1 %while.14 = (s32[]{:T(128)}, f32[1,256,512]{2,1,0:T(8,128)S(1)}, s32[]{:T(128)}, bf16[32,1]{0,1:T(2,128)(2,1)S(1)}, bf16[32,1,256,512]{3,2,1,0:T(8,128)(2,1)}, /*index=5*/s32[]{:T(128)}, s32[]{:T(128)}) while((s32[]{:T(128)}, f32[1,256,512]{2,1,0:T(8,128)S(1)}, s32[]{:T(128)}, bf16[32,1]{0,1:T(2,128)(2,1)S(1)}, ...), condition=%wide.region_6.7_spmd.clone, body=%wide.region_5.6_spmd.clone.sunk | while | flops 655365 | bytes 1310839 | solution.py:33
  267.9 1.3 fusion.42
  270.5 1.3 fusion.42
  273.0 1.3 fusion.42
  275.5 1.3 fusion.42
  278.1 1.3 fusion.42
  280.6 1.3 fusion.42
  283.1 1.3 fusion.42
  285.7 1.3 fusion.42
  288.2 1.3 fusion.42
  290.7 1.3 fusion.42
  293.3 1.3 fusion.42
  295.8 1.3 fusion.42
  298.3 1.3 fusion.42
  300.9 1.3 fusion.42
  303.4 1.3 fusion.42
  305.9 1.3 fusion.42
  308.5 1.3 fusion.42
  311.0 1.3 fusion.42
  313.5 1.3 fusion.42
  316.1 1.3 fusion.42
  318.6 1.3 fusion.42
  321.1 1.3 fusion.42
  323.7 1.3 fusion.42
  326.2 1.3 fusion.42
  328.8 1.3 fusion.42
  331.3 1.3 fusion.42
  333.8 1.3 fusion.42
  336.4 1.3 fusion.42
  338.9 1.3 fusion.42
  341.4 1.3 fusion.42
  344.0 1.3 fusion.42
  346.5 1.3 fusion.42
  347.8 3.2 fusion.37
  351.7 7.7 %convolution_convert_fusion = bf16[768,4096]{1,0:T(8,128)(2,1)} fusion(bf16[512,4096]{1,0:T(8,128)(2,1)} %all-gather.10.cloned.1.call-done, f32[768,512]{0,1:T(8,128)S(1)} %get-tuple-element.142, f32[512]{0:T(512)S(1)} %copy-done.5, f32[768]{0:T(1024)S(1)} %add_rsqrt_fusion, f32[768]{0:T(1024)S(1)} %broadcast_multiply_fusion), kind=kOutput, calls=%fused_computation.3 | convolution fusion | flops 3225944064 | bytes 12066816 | tf_op jit(solution)/shard_map/dot_general | solution.py:138
  359.5 42.9 %reduce-scatter.2.cloned.1.call-done = bf16[96,4096]{1,0:T(8,128)(2,1)} async-done(((bf16[768,4096]{1,0:T(8,128)(2,1)}), bf16[96,4096]{1,0:T(8,128)(2,1)}) %reduce-scatter.2.cloned.1.call-update) | async-done | bytes 786448 | tf_op jit(solution)/shard_map/reduce_scatter | solution.py:137
  402.4 2.2 fusion.5
  (78 shorter events, 23.9 us)
Async XLA Ops:
  6.5 5.2 %copy-start.4 = (s32[1,768]{1,0:T(1,128)S(1)}, s32[1,768]{1,0:T(1,128)}, u32[]{:S(2)}) copy-start(s32[1,768]{1,0:T(1,128)} %param.17) | copy-start | bytes 9220
  6.5 5.6 %copy-start.2 = (s32[768]{0:T(1024)S(1)}, s32[768]{0:T(1024)}, u32[]{:S(2)}) copy-start(s32[768]{0:T(1024)} %param.19) | copy-start | bytes 9220
  6.5 51.6 %all-gather.6.cloned.1.call-start = ((), (), s32[]{:S(2)}) async-start(), calls=%async_computation.1 | async-start | bytes 7077888 | tf_op jit(solution)/shard_map/all_gather | solution.py:99
  8.0 6.2 %copy-start.3 = (s32[1,768]{1,0:T(1,128)S(1)}, s32[1,768]{1,0:T(1,128)}, u32[]{:S(2)}) copy-start(s32[1,768]{1,0:T(1,128)} %param.16) | copy-start | bytes 9220
  10.3 148.3 %all-gather.8.cloned.1.call-start = ((), (), s32[]{:S(2)}) async-start(), calls=%async_computation.2 | async-start | bytes 8650752 | tf_op jit(solution)/shard_map/all_gather | solution.py:100
  11.0 255.7 %all-gather.12.cloned.1.call-start = ((), (), s32[]{:S(2)}) async-start(), calls=%async_computation.5 | async-start | bytes 8650752 | tf_op jit(solution)/shard_map/all_gather | solution.py:16
  169.5 64.7 %copy-start.1 = (bf16[768,1024]{1,0:T(8,128)(2,1)}, bf16[768,1024]{1,0:T(8,128)(2,1)S(1)}, u32[]{:S(2)}) copy-start(bf16[768,1024]{1,0:T(8,128)(2,1)S(1)} %convolution_convert_fusion.1) | copy-start | bytes 4718596
  169.5 3.3 copy-start.6
  170.8 180.5 %all-gather.10.cloned.1.call-start = ((), (), s32[]{:S(2)}) async-start(), calls=%async_computation.3 | async-start | bytes 4325376 | tf_op jit(solution)/shard_map/all_gather | solution.py:136
  171.4 231.0 %reduce-scatter.2.cloned.1.call-start = ((), (), s32[]{:S(2)}) async-start(), calls=%async_computation.4 | async-start | bytes 7077888 | tf_op jit(solution)/shard_map/reduce_scatter | solution.py:137
  351.0 0.7 copy-start.5
  359.4 42.9 %copy-start = (bf16[96,4096]{1,0:T(8,128)(2,1)S(1)}, bf16[96,4096]{1,0:T(8,128)(2,1)}, u32[]{:S(2)}) copy-start(bf16[96,4096]{1,0:T(8,128)(2,1)} %param.11) | copy-start | bytes 2359300
Sparse Core Ops, SparseCore 0:
  10.4 47.6 all-gather.5
  60.7 97.8 all-gather.7
  170.9 95.7 all-gather.11
  269.0 77.5 all-gather.9
  359.6 42.7 reduce-scatter.1
where the time goes:
time: 413 us; the launch traced here: 411 us
  waiting for transfers between devices  220 us (53%)
  blocking collectives  57.4 us (14%)
  other arithmetic  48.8 us (12%)
  matrix products  25.7 us (6%)
  local copies, waits for them, and re-layouts  22.3 us (5%)
  loops' own time  21.7 us (5%)
  between operations  15.3 us (4%)
    all_gather x1, waiting for transfers between devices, local(): parameter_collection = lax.all_gather(w_qkv, 'ctx', axis=0, tiled=True)  100 us
    unnamed x1, blocking collectives  57.4 us
    reduce_scatter x1, waiting for transfers between devices, local(): lax.psum_scatter(jnp.dot(normed_heads, out_columns, preferred_element_typ...  42.9 us
    all_gather x1, waiting for transfers between devices, local(): every_row_list = lax.all_gather(normed, 'tp', axis=0, tiled=True)  42.6 us
    select_n x32, other arithmetic, hop(): return jax.tree.map(lambda a, b: jnp.where(reached, a, b), new, before)  40.6 us
    all_gather x1, waiting for transfers between devices, carried_in(): lax.all_gather(part.astype(kind), axis)  32.5 us
    another operation x1, loops' own time, carried_in(): return lax.fori_loop(0, count, hop, start)  21.7 us
    dynamic_slice x32, local copies, waits for them, and re-layouts, hop(): part[k].astype(own.dtype)  18.7 us
  transfers between devices with their start and end apart: 5, of which 4 were waited for; matrix products, arithmetic and copies ran while one was open for 17% of the time, Pallas kernels for 0%

commit v1 on v0

--- a/solution.py
+++ b/solution.py
@@ -96,7 +96,12 @@
     document_begin_flags,
 ):
     normed = rms_rows(tokens, norm_gain)
-    every_row_list = lax.all_gather(normed, "tp", axis=0, tiled=True)
+    ring = [normed]
+    for hop_ in range(7):
+        ring.append(lax.ppermute(ring[-1], "tp", [(dev, (dev + 1) % 8) for dev in range(8)]))
+    every_row_list = jnp.roll(
+        jnp.concatenate(ring[::-1], axis=0), (lax.axis_index("tp") + 1) * ring[0].shape[0], axis=0
+    )
     parameter_collection = lax.all_gather(w_qkv, "ctx", axis=0, tiled=True)
     rows_combined = jnp.dot(
         every_row_list, parameter_collection, preferred_element_type=jnp.float32

time: 413 us -> 380 us (0.920)
  waiting for transfers between devices: 220 us -> 142 us
  local copies, waits for them, and re-layouts: 22.3 us -> 42.1 us
  starting transfers between devices: 0.16 us -> 17.7 us
  blocking collectives: 57.4 us -> 63.8 us
    all_gather x1, waiting for transfers between devices: 100 us -> 0.01 us  [local(): parameter_collection = lax.all_gather(w_qkv, 'ctx', axis=0, tiled=True)]
    ppermute x0 -> x7, waiting for transfers between devices: none -> 59.7 us  [local(): lax.ppermute(ring[-1], 'tp', [(dev, (dev + 1) % 8) for dev in range(8)])]
    all_gather x1 -> x0, waiting for transfers between devices: 42.6 us -> none  [local(): every_row_list = lax.all_gather(normed, 'tp', axis=0, tiled=True)]
    unnamed x17 -> x37, local copies, waits for them, and re-layouts: 1.84 us -> 21.7 us
    ppermute x0 -> x7, starting transfers between devices: none -> 17.6 us  [local(): lax.ppermute(ring[-1], 'tp', [(dev, (dev + 1) % 8) for dev in range(8)])]
    unnamed x1, blocking collectives: 57.4 us -> 63.8 us
    all_gather x1, waiting for transfers between devices: 32.5 us -> 37.4 us  [carried_in(): lax.all_gather(part.astype(kind), axis)]
  transfers between devices with their start and end apart: 5 -> 11, of which waited for: 4 -> 9; matrix products, arithmetic and copies ran while one was open for 17% -> 25% of each run, Pallas kernels for 0% -> 0%
where the time goes in v1:
time: 380 us; the launch traced here: 378 us
  waiting for transfers between devices  142 us (37%)
  blocking collectives  63.8 us (17%)
  other arithmetic  50.2 us (13%)
  local copies, waits for them, and re-layouts  42.1 us (11%)
  matrix products  25.7 us (7%)
  loops' own time  21.7 us (6%)
  starting transfers between devices  17.7 us (5%)
  between operations  15.3 us (4%)
    unnamed x1, blocking collectives  63.8 us
    ppermute x7, waiting for transfers between devices, local(): lax.ppermute(ring[-1], 'tp', [(dev, (dev + 1) % 8) for dev in range(8)])  59.7 us
    reduce_scatter x1, waiting for transfers between devices, local(): lax.psum_scatter(jnp.dot(normed_heads, out_columns, preferred_element_typ...  43.4 us
    select_n x32, other arithmetic, hop(): return jax.tree.map(lambda a, b: jnp.where(reached, a, b), new, before)  40.6 us
    all_gather x1, waiting for transfers between devices, carried_in(): lax.all_gather(part.astype(kind), axis)  37.4 us
    another operation x1, loops' own time, carried_in(): return lax.fori_loop(0, count, hop, start)  21.7 us
    unnamed x37, local copies, waits for them, and re-layouts  21.7 us
    dynamic_slice x32, local copies, waits for them, and re-layouts, hop(): part[k].astype(own.dtype)  18.7 us
  transfers between devices with their start and end apart: 11, of which 9 were waited for; matrix products, arithmetic and copies ran while one was open for 25% of the time, Pallas kernels for 0%

profile of v1, /device:TPU:1, one launch (start us, length us, event | category | flops | bytes accessed | tf_op | source)
XLA Modules:
  0.0 378.4 jit_solution(820193846971510509)
XLA Ops:
  7.3 1.4 fusion.7
  8.7 1.4 fusion.9
  10.1 2.6 collective-permute-start
  12.7 8.9 %collective-permute-done = bf16[96,4096]{1,0:T(8,128)(2,1)S(1)} collective-permute-done((bf16[96,4096]{1,0:T(8,128)(2,1)S(1)}, bf16[96,4096]{1,0:T(8,128)(2,1)S(1)}, u32[]{:S(2)}, u32[]{:S(2)}) %collective-permute-start) | collective-permute-done | bytes 786464 | tf_op jit(solution)/shard_map/ppermute | solution.py:101
  21.7 2.5 collective-permute-start.1
  24.1 8.9 %collective-permute-done.1 = bf16[96,4096]{1,0:T(8,128)(2,1)S(1)} collective-permute-done((bf16[96,4096]{1,0:T(8,128)(2,1)S(1)}, bf16[96,4096]{1,0:T(8,128)(2,1)S(1)}, u32[]{:S(2)}, u32[]{:S(2)}) %collective-permute-start.1) | collective-permute-done | bytes 786464 | tf_op jit(solution)/shard_map/ppermute | solution.py:101
  33.1 2.5 collective-permute-start.2
  35.6 8.9 %collective-permute-done.2 = bf16[96,4096]{1,0:T(8,128)(2,1)S(1)} collective-permute-done((bf16[96,4096]{1,0:T(8,128)(2,1)S(1)}, bf16[96,4096]{1,0:T(8,128)(2,1)S(1)}, u32[]{:S(2)}, u32[]{:S(2)}) %collective-permute-start.2) | collective-permute-done | bytes 786464 | tf_op jit(solution)/shard_map/ppermute | solution.py:101
  44.5 2.5 collective-permute-start.3
  47.0 8.9 %collective-permute-done.3 = bf16[96,4096]{1,0:T(8,128)(2,1)S(1)} collective-permute-done((bf16[96,4096]{1,0:T(8,128)(2,1)S(1)}, bf16[96,4096]{1,0:T(8,128)(2,1)S(1)}, u32[]{:S(2)}, u32[]{:S(2)}) %collective-permute-start.3) | collective-permute-done | bytes 786464 | tf_op jit(solution)/shard_map/ppermute | solution.py:101
  55.9 2.5 collective-permute-start.4
  58.4 8.9 %collective-permute-done.4 = bf16[96,4096]{1,0:T(8,128)(2,1)} collective-permute-done((bf16[96,4096]{1,0:T(8,128)(2,1)S(1)}, bf16[96,4096]{1,0:T(8,128)(2,1)}, u32[]{:S(2)}, u32[]{:S(2)}) %collective-permute-start.4) | collective-permute-done | bytes 786464 | tf_op jit(solution)/shard_map/ppermute | solution.py:101
  67.3 2.6 collective-permute-start.5
  71.0 8.2 %collective-permute-done.5 = bf16[96,4096]{1,0:T(8,128)(2,1)} collective-permute-done((bf16[96,4096]{1,0:T(8,128)(2,1)}, bf16[96,4096]{1,0:T(8,128)(2,1)}, u32[]{:S(2)}, u32[]{:S(2)}) %collective-permute-start.5) | collective-permute-done | bytes 786464 | tf_op jit(solution)/shard_map/ppermute | solution.py:101
  79.2 2.5 collective-permute-start.6
  84.9 6.8 %collective-permute-done.6 = bf16[96,4096]{1,0:T(8,128)(2,1)} collective-permute-done((bf16[96,4096]{1,0:T(8,128)(2,1)}, bf16[96,4096]{1,0:T(8,128)(2,1)}, u32[]{:S(2)}, u32[]{:S(2)}) %collective-permute-start.6) | collective-permute-done | bytes 786464 | tf_op jit(solution)/shard_map/ppermute | solution.py:101
  91.7 2.1 constant_dynamic-update-slice_fusion.15
  93.8 2.1 constant_dynamic-update-slice_fusion.14
  95.9 2.1 constant_dynamic-update-slice_fusion.13
  103.0 2.2 constant_dynamic-update-slice_fusion.7
  105.1 2.1 constant_dynamic-update-slice_fusion.6
  107.2 2.1 constant_dynamic-update-slice_fusion.5
  114.3 11.0 %fusion.4 = bf16[768,1024]{1,0:T(8,128)(2,1)S(1)} fusion(bf16[4096,1024]{1,0:T(8,128)(2,1)} %all-gather.5.cloned.1.call-done, bf16[1536,4096]{1,0:T(8,128)(2,1)} %constant_dynamic-update-slice_fusion, s32[]{:T(128)S(6)} %select_n.65), kind=kOutput, calls=%fused_computation.12 | convolution fusion | flops 6443237376 | bytes 16252932 | tf_op jit(solution)/shard_map/dot_general | solution.py:106
  125.3 1.3 convolution_convert_fusion.1
  130.1 63.8 %all-reduce = bf16[32]{0:T(256)(128)(2,1)S(1)} all-reduce(bf16[32]{0:T(256)(128)(2,1)S(1)} %dynamic-update-slice), channel_id=1, replica_groups=mesh['ctx'=32,'tp'=8] {'ctx'}, use_global_device_ids=true, to_apply=%add | all-reduce | flops 32 | bytes 128
  193.9 2.5 fusion.11
  196.5 37.4 %all-gather.9.cloned.1.call-done = bf16[8192,512]{1,0:T(8,128)(2,1)} async-done(((bf16[256,512]{1,0:T(8,128)(2,1)}), bf16[8192,512]{1,0:T(8,128)(2,1)}) %all-gather.9.cloned.1.call-update) | async-done | bytes 8388624 | tf_op jit(solution)/shard_map/all_gather | solution.py:16
  233.9 81.1 %while.14 = (s32[]{:T(128)}, f32[1,256,512]{2,1,0:T(8,128)S(1)}, s32[]{:T(128)}, bf16[32,1]{0,1:T(2,128)(2,1)S(1)}, bf16[32,1,256,512]{3,2,1,0:T(8,128)(2,1)}, /*index=5*/s32[]{:T(128)}, s32[]{:T(128)}) while((s32[]{:T(128)}, f32[1,256,512]{2,1,0:T(8,128)S(1)}, s32[]{:T(128)}, bf16[32,1]{0,1:T(2,128)(2,1)S(1)}, ...), condition=%wide.region_6.7_spmd.clone, body=%wide.region_5.6_spmd.clone.sunk | while | flops 655365 | bytes 1310839 | solution.py:33
  235.1 1.3 fusion.47
  237.6 1.3 fusion.47
  240.2 1.3 fusion.47
  242.7 1.3 fusion.47
  245.2 1.3 fusion.47
  247.8 1.3 fusion.47
  250.3 1.3 fusion.47
  252.8 1.3 fusion.47
  255.4 1.3 fusion.47
  257.9 1.3 fusion.47
  260.4 1.3 fusion.47
  283.2 1.3 fusion.47
  293.4 1.3 fusion.47
  298.5 1.3 fusion.47
  301.0 1.3 fusion.47
  311.1 1.3 fusion.47
  315.0 3.2 fusion.43
  318.4 7.8 %convolution_convert_fusion = bf16[768,4096]{1,0:T(8,128)(2,1)} fusion(bf16[512,4096]{1,0:T(8,128)(2,1)} %all-gather.7.cloned.1.call-done, f32[768,512]{0,1:T(8,128)S(1)} %get-tuple-element.142, f32[512]{0:T(512)S(1)} %copy-done.8, f32[768]{0:T(1024)S(1)} %add_rsqrt_fusion, f32[768]{0:T(1024)S(1)} %broadcast_multiply_fusion), kind=kOutput, calls=%fused_computation.3 | convolution fusion | flops 3225944064 | bytes 12066816 | tf_op jit(solution)/shard_map/dot_general | solution.py:143
  326.2 43.4 %reduce-scatter.2.cloned.1.call-done = bf16[96,4096]{1,0:T(8,128)(2,1)} async-done(((bf16[768,4096]{1,0:T(8,128)(2,1)}), bf16[96,4096]{1,0:T(8,128)(2,1)}) %reduce-scatter.2.cloned.1.call-update) | async-done | bytes 786448 | tf_op jit(solution)/shard_map/reduce_scatter | solution.py:142
  369.6 2.2 fusion.10
  (111 shorter events, 55.9 us)
Async XLA Ops:
  6.5 64.0 %copy-start.7 = (s32[1,768]{1,0:T(1,128)S(1)}, s32[1,768]{1,0:T(1,128)}, u32[]{:S(2)}) copy-start(s32[1,768]{1,0:T(1,128)} %param.17) | copy-start | bytes 9220
  6.5 75.1 %copy-start.5 = (s32[768]{0:T(1024)S(1)}, s32[768]{0:T(1024)}, u32[]{:S(2)}) copy-start(s32[768]{0:T(1024)} %param.19) | copy-start | bytes 9220
  6.5 77.1 %copy-start.6 = (s32[1,768]{1,0:T(1,128)S(1)}, s32[1,768]{1,0:T(1,128)}, u32[]{:S(2)}) copy-start(s32[1,768]{1,0:T(1,128)} %param.16) | copy-start | bytes 9220
  6.5 107.8 %all-gather.5.cloned.1.call-start = ((), (), s32[]{:S(2)}) async-start(), calls=%async_computation.1 | async-start | bytes 8650752 | tf_op jit(solution)/shard_map/all_gather | solution.py:105
  7.3 226.6 %all-gather.9.cloned.1.call-start = ((), (), s32[]{:S(2)}) async-start(), calls=%async_computation.4 | async-start | bytes 8650752 | tf_op jit(solution)/shard_map/all_gather | solution.py:16
  10.1 11.5 %collective-permute-start = (bf16[96,4096]{1,0:T(8,128)(2,1)S(1)}, bf16[96,4096]{1,0:T(8,128)(2,1)S(1)}, u32[]{:S(2)}, u32[]{:S(2)}) collective-permute-start(bf16[96,4096]{1,0:T(8,128)(2,1)S(1)} %fusion.9), channel_id=1, source_target_pairs={{0,1},{1,2},{2,3},{3,4},{4,5},{5,6},{6,7},{7,0},{8,9},{9,10},{10,1... | collective-permute-start | bytes 2359304 | tf_op jit(solution)/shard_map/ppermute | solution.py:101
  21.7 11.4 %collective-permute-start.1 = (bf16[96,4096]{1,0:T(8,128)(2,1)S(1)}, bf16[96,4096]{1,0:T(8,128)(2,1)S(1)}, u32[]{:S(2)}, u32[]{:S(2)}) collective-permute-start(bf16[96,4096]{1,0:T(8,128)(2,1)S(1)} %collective-permute-done), channel_id=1, source_target_pairs={{0,1},{1,2},{2,3},{3,4},{4,5},{5,6},{6,7},{7,0},{8,9},{9,10},{10,1... | collective-permute-start | bytes 2359304 | tf_op jit(solution)/shard_map/ppermute | solution.py:101
  33.1 11.4 %collective-permute-start.2 = (bf16[96,4096]{1,0:T(8,128)(2,1)S(1)}, bf16[96,4096]{1,0:T(8,128)(2,1)S(1)}, u32[]{:S(2)}, u32[]{:S(2)}) collective-permute-start(bf16[96,4096]{1,0:T(8,128)(2,1)S(1)} %collective-permute-done.1), channel_id=1, source_target_pairs={{0,1},{1,2},{2,3},{3,4},{4,5},{5,6},{6,7},{7,0},{8,9},{9,10},{10,1... | collective-permute-start | bytes 2359304 | tf_op jit(solution)/shard_map/ppermute | solution.py:101
  44.5 11.4 %collective-permute-start.3 = (bf16[96,4096]{1,0:T(8,128)(2,1)S(1)}, bf16[96,4096]{1,0:T(8,128)(2,1)S(1)}, u32[]{:S(2)}, u32[]{:S(2)}) collective-permute-start(bf16[96,4096]{1,0:T(8,128)(2,1)S(1)} %collective-permute-done.2), channel_id=1, source_target_pairs={{0,1},{1,2},{2,3},{3,4},{4,5},{5,6},{6,7},{7,0},{8,9},{9,10},{10,1... | collective-permute-start | bytes 2359304 | tf_op jit(solution)/shard_map/ppermute | solution.py:101
  55.9 42.1 %copy-start.1 = (bf16[96,4096]{1,0:T(8,128)(2,1)}, bf16[96,4096]{1,0:T(8,128)(2,1)S(1)}, u32[]{:S(2)}) copy-start(bf16[96,4096]{1,0:T(8,128)(2,1)S(1)} %collective-permute-done.3) | copy-start | bytes 2359300
  55.9 11.4 %collective-permute-start.4 = (bf16[96,4096]{1,0:T(8,128)(2,1)S(1)}, bf16[96,4096]{1,0:T(8,128)(2,1)}, u32[]{:S(2)}, u32[]{:S(2)}) collective-permute-start(bf16[96,4096]{1,0:T(8,128)(2,1)S(1)} %collective-permute-done.3), channel_id=1, source_target_pairs={{0,1},{1,2},{2,3},{3,4},{4,5},{5,6},{6,7},{7,0},{8,9},{9,10},{10,1... | collective-permute-start | bytes 2359304 | tf_op jit(solution)/shard_map/ppermute | solution.py:101
  67.3 11.8 %collective-permute-start.5 = (bf16[96,4096]{1,0:T(8,128)(2,1)}, bf16[96,4096]{1,0:T(8,128)(2,1)}, u32[]{:S(2)}, u32[]{:S(2)}) collective-permute-start(bf16[96,4096]{1,0:T(8,128)(2,1)} %collective-permute-done.4), channel_id=1, source_target_pairs={{0,1},{1,2},{2,3},{3,4},{4,5},{5,6},{6,7},{7,0},{8,9},{9,10},{10,1... | collective-permute-start | bytes 2359304 | tf_op jit(solution)/shard_map/ppermute | solution.py:101
  79.2 12.5 %collective-permute-start.6 = (bf16[96,4096]{1,0:T(8,128)(2,1)}, bf16[96,4096]{1,0:T(8,128)(2,1)}, u32[]{:S(2)}, u32[]{:S(2)}) collective-permute-start(bf16[96,4096]{1,0:T(8,128)(2,1)} %collective-permute-done.5), channel_id=1, source_target_pairs={{0,1},{1,2},{2,3},{3,4},{4,5},{5,6},{6,7},{7,0},{8,9},{9,10},{10,1... | collective-permute-start | bytes 2359304 | tf_op jit(solution)/shard_map/ppermute | solution.py:101
  98.9 2.8 copy-start
  98.9 2.8 copy-start.3
  103.0 6.3 %copy-start.2 = (bf16[96,4096]{1,0:T(8,128)(2,1)S(1)}, bf16[96,4096]{1,0:T(8,128)(2,1)}, u32[]{:S(2)}) copy-start(bf16[96,4096]{1,0:T(8,128)(2,1)} %copy-done.1) | copy-start | bytes 2359300
  125.3 71.2 %copy-start.4 = (bf16[768,1024]{1,0:T(8,128)(2,1)}, bf16[768,1024]{1,0:T(8,128)(2,1)S(1)}, u32[]{:S(2)}) copy-start(bf16[768,1024]{1,0:T(8,128)(2,1)S(1)} %fusion.4) | copy-start | bytes 4718596
  125.3 3.4 copy-start.9
  126.6 191.8 %all-gather.7.cloned.1.call-start = ((), (), s32[]{:S(2)}) async-start(), calls=%async_computation.2 | async-start | bytes 4325376 | tf_op jit(solution)/shard_map/all_gather | solution.py:141
  127.4 242.2 %reduce-scatter.2.cloned.1.call-start = ((), (), s32[]{:S(2)}) async-start(), calls=%async_computation.3 | async-start | bytes 7077888 | tf_op jit(solution)/shard_map/reduce_scatter | solution.py:142
  315.0 3.5 copy-start.8
Sparse Core Ops, SparseCore 0:
  9.9 101.9 all-gather.4
  126.8 107.0 all-gather.8
  236.3 77.5 all-gather.6
  326.4 43.2 reduce-scatter.1
